TPU v7x, 32 devices: a whole 2x2x4 slice. The times are simulated.
32 devices in a mesh: seg: 8 (over z, x), head: 4 (over y, core).
Axes of the slice: x: 2, y: 2, z: 4, core: 2. Of those that a mesh axis runs over, the one named last changes fastest.
Arguments:
- q_heads: bfloat16 [6144, 2048], P('seg', 'head'), may hold values from -6 to 6
- k_heads: bfloat16 [6144, 2048], P('seg', 'head'), may hold values from -6 to 6
- v_heads: bfloat16 [6144, 2048], P('seg', 'head'), may hold values from -600 to 600
- log_decay: float32 [16, 6144], P('head', 'seg'), may hold values from -1 to 0
- parent: int32 [8], replicated, may hold values from -1 to 7, as said below
- norm_gain: float32 [2048], P('head'), may hold values from 0.1 to 1.9
- w_out: bfloat16 [2048, 6144], P('head'), may hold values from -0.125 to 0.125
Outputs:
- mixed: bfloat16 [6144, 6144], P(('seg', 'head'))
Inputs may be any that keep to these rules, and one draw needn't show every extreme that they name: A segment's parent is a root or a segment whose parent is a root; the tree has three levels, and the third is never empty.
All inputs are finite; a program needn't handle non-finite values.
Results may differ from a plain program's by a relative error of at most 0.0051.
Values sent between devices are 32-bit elements; how exact they have to be, the bound alone decides.
A program may use at most 128 MiB of HBM per device.

v0:
```python
import jax
import jax.numpy as jnp
from jax import lax
from jax.sharding import PartitionSpec as P


def per_device(q_heads, k_heads, v_heads, log_decay, parent, norm_gain, w_out):
    segment_len = q_heads.shape[0]
    head_count = log_decay.shape[0]
    head_width = q_heads.shape[1] // head_count
    queries = q_heads.reshape(segment_len, head_count, head_width)
    key_rows = k_heads.reshape(segment_len, head_count, head_width)
    values = v_heads.reshape(segment_len, head_count, head_width)
    running = jnp.cumsum(log_decay, axis=1)
    segment_total = running[:, -1]
    key_weight = jnp.exp(segment_total[:, None] - running)
    weighted = key_rows.astype(jnp.float32) * key_weight.T[:, :, None]
    local_state = jnp.einsum(
        "shd,she->hde", weighted, values.astype(jnp.float32), precision=lax.Precision.HIGHEST
    )
    scores = jnp.einsum("thd,shd->hts", queries, key_rows, preferred_element_type=jnp.float32)
    row_index = lax.broadcasted_iota(jnp.int32, (segment_len, segment_len), 0)
    col_index = lax.broadcasted_iota(jnp.int32, (segment_len, segment_len), 1)
    causal = row_index >= col_index
    log_gap = running[:, :, None] - running[:, None, :]
    decay_factor = jnp.where(causal[None], jnp.exp(jnp.minimum(log_gap, 0.0)), 0.0)
    weights = (scores * head_width ** (-0.5) * decay_factor).astype(jnp.bfloat16)
    within = jnp.einsum("hts,she->the", weights, values, preferred_element_type=jnp.float32)
    own_index = lax.axis_index("seg")
    parent_id = parent[own_index]
    grand_id = jnp.where(parent_id >= 0, parent[jnp.maximum(parent_id, 0)], -1)
    states = lax.all_gather(local_state[None], "seg", axis=0, tiled=True)
    totals = lax.all_gather(segment_total[None], "seg", axis=0, tiled=True)
    segment_ids = jnp.arange(states.shape[0], dtype=jnp.int32)
    is_parent = segment_ids == parent_id
    is_grand = segment_ids == grand_id
    parent_sum = jnp.sum(jnp.where(is_parent[:, None, None, None], states, 0.0), axis=0)
    grand_sum = jnp.sum(jnp.where(is_grand[:, None, None, None], states, 0.0), axis=0)
    parent_total = jnp.sum(jnp.where(is_parent[:, None], totals, 0.0), axis=0)
    parent_sum, grand_sum, parent_total = (parent_sum, grand_sum, parent_total)
    prefix = jnp.exp(parent_total)[:, None, None] * grand_sum + parent_sum
    prefix_term = (
        jnp.einsum(
            "thd,hde->the", queries.astype(jnp.float32), prefix, precision=lax.Precision.HIGHEST
        )
        * jnp.exp(running).T[:, :, None]
    )
    attention = (prefix_term + within).reshape(segment_len, head_count * head_width)
    squares = lax.psum(jnp.sum(attention * attention, axis=1), "head")
    total_features = head_count * head_width * lax.axis_size("head")
    inverse = 1.0 / jnp.sqrt(squares / total_features + 1e-06)
    normed = (attention * inverse[:, None] * norm_gain[None, :]).astype(jnp.bfloat16)
    mixed = lax.psum_scatter(
        jnp.dot(normed, w_out, preferred_element_type=jnp.float32),
        "head",
        scatter_dimension=0,
        tiled=True,
    )
    return mixed.astype(jnp.bfloat16)


def solution(mesh):
    return jax.shard_map(
        per_device,
        mesh=mesh,
        in_specs=(
            P("seg", "head"),
            P("seg", "head"),
            P("seg", "head"),
            P("head", "seg"),
            P(),
            P("head"),
            P("head", None),
        ),
        out_specs=P(("seg", "head"), None),
        check_vma=False,
    )
```

profile of v0, /device:TPU:0, one launch (start us, length us, event | category | flops | bytes accessed | tf_op | source)
XLA Modules:
  0.0 234.6 jit_solution(15167253058687618074)
XLA Ops:
  6.5 0.8 reshape.72
  7.3 1.1 reduce-window.6
  8.5 0.2 slice_reduce_fusion
  8.6 0.2 reduce-window.9
  8.8 0.1 add_bitcast_fusion
  8.9 0.2 slice_reduce_fusion.1
  9.1 0.1 exponential_bitcast_fusion.1
  9.2 0.0 copy-start.4
  9.2 1.4 copy.31
  10.6 1.4 copy.32
  12.0 1.7 fusion.6
  13.7 0.0 all-gather.4.cloned.1.call-update
  13.7 0.0 reduce-scatter.2.cloned.1.call-start
  13.8 0.6 dynamic_slice.6
  15.7 0.6 dynamic_slice.7
  16.2 0.6 dynamic-slice
  17.5 0.2 dynamic-update-slice
  17.7 23.5 %all-reduce = f32[32]{0:T(128)S(1)} all-reduce(f32[32]{0:T(128)S(1)} %dynamic-update-slice), channel_id=2, replica_groups=mesh['seg'=8,'head'=4] {'seg'}, use_global_device_ids=true, to_apply=%add | all-reduce | flops 32 | bytes 256
  41.2 0.1 reshape.78
  41.3 0.7 iota_compare_fusion.2
  41.9 0.1 select_reduce_fusion.2
  42.6 0.2 iota_compare_fusion
  42.8 5.6 %fusion = f32[4,768,128]{1,2,0:T(8,128)} fusion(bf16[768,4,128]{0,2,1:T(8,128)(2,1)S(1)} %bitcast.52, f32[4,768]{1,0:T(4,128)S(1)} %get-tuple-element.8, pred[768,768]{1,0:T(8,128)(4,1)S(1)} %iota_compare_fusion, bf16[768,4,128]{0,2,1:T(8,128)(2,1)S(1)} %bitcast.50, bf16[768,512]{1,0:T(8,128)(2,1)S(1)} %copy-done), kind=kOutput, calls=%fused_computation.1 | convolution fusion | flops 1222115328 | bytes 4534272 | tf_op jit(solution)/shard_map/hts,she->the/dot_general | solution.py:28
  48.3 17.5 %all-gather.4.cloned.1.call-done = f32[32,128,128]{2,1,0:T(8,128)} async-done(((f32[4,128,128]{2,1,0:T(8,128)}), f32[32,128,128]{2,1,0:T(8,128)}) %all-gather.4.cloned.1.call-update) | async-done | bytes 2097168 | tf_op jit(solution)/shard_map/all_gather | solution.py:32
  65.9 2.1 select_reduce_fusion.1
  68.0 1.1 multiply_reduce_fusion
  69.1 5.7 %psum.7 = f32[768]{0:T(1024)S(1)} all-reduce(f32[768]{0:T(1024)S(1)} %get-tuple-element.9), channel_id=1, replica_groups=mesh['seg'=8,'head'=4] {'head'}, use_global_device_ids=true, to_apply=%region_6.7 | all-reduce | flops 768 | bytes 6144 | tf_op jit(solution)/shard_map/psum | solution.py:49
  74.8 0.2 fusion.5
  75.0 11.9 %fusion.21 = f32[768,6144]{1,0:T(8,128)} fusion(bf16[768,512]{0,1:T(8,128)(2,1)S(1)} %fusion.5, bf16[512,6144]{1,0:T(8,128)(2,1)} %param.13), kind=kOutput, calls=%fused_computation.36 | convolution fusion | flops 4831838208 | bytes 25952256 | tf_op jit(solution)/shard_map/dot_general | solution.py:54
  86.9 0.0 reduce-scatter.2.cloned.1.call-update
  87.0 136.8 %reduce-scatter.2.cloned.1.call-done = f32[192,6144]{1,0:T(8,128)} async-done(((f32[768,6144]{1,0:T(8,128)}), f32[192,6144]{1,0:T(8,128)}) %reduce-scatter.2.cloned.1.call-update) | async-done | bytes 4718608 | tf_op jit(solution)/shard_map/reduce_scatter | solution.py:53
  223.7 4.1 %convert_element_type.17 = bf16[192,6144]{1,0:T(8,128)(2,1)} convert(f32[192,6144]{1,0:T(8,128)} %reduce-scatter.2.cloned.1.call-done) | non-fusion elementwise | flops 1179648 | bytes 7077888 | tf_op jit(solution)/shard_map/convert_element_type | solution.py:59
  (15 shorter events, 0.1 us)
Async XLA Ops:
  6.5 36.2 %copy-start = (bf16[768,512]{1,0:T(8,128)(2,1)S(1)}, bf16[768,512]{1,0:T(8,128)(2,1)}, u32[]{:S(2)}) copy-start(bf16[768,512]{1,0:T(8,128)(2,1)} %param.7) | copy-start | bytes 2359300
  6.5 59.3 %all-gather.4.cloned.1.call-start = ((), (), s32[]{:S(2)}) async-start(), calls=%async_computation.2 | async-start | bytes 2359296 | tf_op jit(solution)/shard_map/all_gather | solution.py:32
  9.2 4.6 %copy-start.3 = (s32[8]{0:T(128)S(1)}, s32[8]{0:T(128)}, u32[]{:S(2)}) copy-start(s32[8]{0:T(128)} %param.11) | copy-start | bytes 100
  9.2 7.1 %copy-start.4 = (u32[32]{0:T(128)S(1)}, u32[32]{0:T(128)}, u32[]{:S(2)}) copy-start(u32[32]{0:T(128)} %constant.29) | copy-start | bytes 388
  13.7 210.0 %reduce-scatter.2.cloned.1.call-start = ((), (), s32[]{:S(2)}) async-start(), calls=%async_computation.1 | async-start | bytes 23592960 | tf_op jit(solution)/shard_map/reduce_scatter | solution.py:53
  65.9 2.1 copy-start.1
  68.0 6.8 %copy-start.2 = (f32[512]{0:T(512)S(1)}, f32[512]{0:T(512)}, u32[]{:S(2)}) copy-start(f32[512]{0:T(512)} %param.12) | copy-start | bytes 6148
Sparse Core Ops, SparseCore 0:
  13.8 51.9 all-gather.3
  87.1 136.6 reduce-scatter.1
where the time goes:
time: 235 us
  waiting for transfers between devices  154 us (66%)
  blocking collectives  29.1 us (12%)
  matrix products  20.2 us (9%)
  between operations  16 us (7%)
  other arithmetic  8.75 us (4%)
  local copies, waits for them, and re-layouts  6.08 us (3%)
    reduce_scatter x1, waiting for transfers between devices, per_device(): lax.psum_scatter(jnp.dot(normed, w_out, preferred_element_type=jnp.float3...  137 us
    unnamed x1, blocking collectives  23.5 us
    all_gather x1, waiting for transfers between devices, per_device(): states = lax.all_gather(local_state[None], 'seg', axis=0, tiled=True)  17.5 us
    dot_general x1, matrix products, per_device(): jnp.dot(normed, w_out, preferred_element_type=jnp.float32)  11.9 us
    psum x1, blocking collectives, per_device(): squares = lax.psum(jnp.sum(attention * attention, axis=1), 'head')  5.67 us
    dot_general x1, matrix products, per_device(): jnp.einsum('hts,she->the', weights, values, preferred_element_type=jnp.fl...  5.55 us
  transfers between devices with their start and end apart: 2, of which 2 were waited for; matrix products, arithmetic and copies ran while one was open for 4% of the time, Pallas kernels for 0%

commit v1 on v0

--- a/solution.py
+++ b/solution.py
@@ -29,7 +29,12 @@
     own_index = lax.axis_index("seg")
     parent_id = parent[own_index]
     grand_id = jnp.where(parent_id >= 0, parent[jnp.maximum(parent_id, 0)], -1)
-    states = lax.all_gather(local_state[None], "seg", axis=0, tiled=True)
+    ring = [local_state[None]]
+    for hop in range(7):
+        ring.append(lax.ppermute(ring[-1], "seg", [(dev, (dev + 1) % 8) for dev in range(8)]))
+    states = jnp.roll(
+        jnp.concatenate(ring[::-1], axis=0), (lax.axis_index("seg") + 1) * ring[0].shape[0], axis=0
+    )
     totals = lax.all_gather(segment_total[None], "seg", axis=0, tiled=True)
     segment_ids = jnp.arange(states.shape[0], dtype=jnp.int32)
     is_parent = segment_ids == parent_id

time: 235 us -> 271 us (1.15)
  waiting for transfers between devices: 154 us -> 184 us
  local copies, waits for them, and re-layouts: 6.08 us -> 12.1 us
  starting transfers between devices: 0.04 us -> 3.04 us
    ppermute x0 -> x7, waiting for transfers between devices: none -> 48.4 us  [per_device(): lax.ppermute(ring[-1], 'seg', [(dev, (dev + 1) % 8) for dev in range(8)])]
    all_gather x1 -> x0, waiting for transfers between devices: 17.5 us -> none  [per_device(): states = lax.all_gather(local_state[None], 'seg', axis=0, tiled=True)]
    unnamed x13 -> x32, local copies, waits for them, and re-layouts: 0.86 us -> 6.68 us
    ppermute x0 -> x7, starting transfers between devices: none -> 3.03 us  [per_device(): lax.ppermute(ring[-1], 'seg', [(dev, (dev + 1) % 8) for dev in range(8)])]
  transfers between devices with their start and end apart: 2 -> 8, of which waited for: 2 -> 7; matrix products, arithmetic and copies ran while one was open for 4% -> 4% of each run, Pallas kernels for 0% -> 0%
where the time goes in v1:
time: 271 us
  waiting for transfers between devices  184 us (68%)
  blocking collectives  27.5 us (10%)
  matrix products  20.6 us (8%)
  between operations  16.3 us (6%)
  local copies, waits for them, and re-layouts  12.1 us (4%)
  other arithmetic  7.85 us (3%)
  starting transfers between devices  3.04 us (1%)
    reduce_scatter x1, waiting for transfers between devices, per_device(): lax.psum_scatter(jnp.dot(normed, w_out, preferred_element_type=jnp.float3...  135 us
    ppermute x7, waiting for transfers between devices, per_device(): lax.ppermute(ring[-1], 'seg', [(dev, (dev + 1) % 8) for dev in range(8)])  48.4 us
    unnamed x1, blocking collectives  21.8 us
    dot_general x1, matrix products, per_device(): jnp.dot(normed, w_out, preferred_element_type=jnp.float32)  11.9 us
    unnamed x32, local copies, waits for them, and re-layouts  6.68 us
    dot_general x1, matrix products, per_device(): jnp.einsum('hts,she->the', weights, values, preferred_element_type=jnp.fl...  6.63 us
    psum x1, blocking collectives, per_device(): squares = lax.psum(jnp.sum(attention * attention, axis=1), 'head')  5.67 us
  transfers between devices with their start and end apart: 8, of which 7 were waited for; matrix products, arithmetic and copies ran while one was open for 4% of the time, Pallas kernels for 0%

profile of v1, /device:TPU:0, one launch (start us, length us, event | category | flops | bytes accessed | tf_op | source)
XLA Modules:
  0.0 270.9 jit_solution(12039541505339274029)
XLA Ops:
  6.5 0.8 reshape.72
  7.3 1.1 reduce-window.6
  9.2 1.4 copy.31
  10.6 1.4 copy.32
  12.0 0.9 fusion.9
  12.9 3.0 %collective-permute-start = (f32[1,4,128,128]{3,2,1,0:T(8,128)S(1)}, f32[1,4,128,128]{3,2,1,0:T(8,128)S(1)}, u32[]{:S(2)}, u32[]{:S(2)}) collective-permute-start(f32[1,4,128,128]{3,2,1,0:T(8,128)S(1)} %fusion.9), channel_id=1, source_target_pairs={{0,4},{4,8},{8,12},{12,16},{16,20},{20,24},{24,28},{28,0},{1,5},{5... | collective-permute-start | bytes 786440 | tf_op jit(solution)/shard_map/ppermute | solution.py:34
  15.9 9.3 %collective-permute-done = f32[1,4,128,128]{3,2,1,0:T(8,128)S(1)} collective-permute-done((f32[1,4,128,128]{3,2,1,0:T(8,128)S(1)}, f32[1,4,128,128]{3,2,1,0:T(8,128)S(1)}, u32[]{:S(2)}, u32[]{:S(2)}) %collective-permute-start) | collective-permute-done | bytes 262176 | tf_op jit(solution)/shard_map/ppermute | solution.py:34
  25.3 10.2 %collective-permute-done.1 = f32[1,4,128,128]{3,2,1,0:T(8,128)S(1)} collective-permute-done((f32[1,4,128,128]{3,2,1,0:T(8,128)S(1)}, f32[1,4,128,128]{3,2,1,0:T(8,128)S(1)}, u32[]{:S(2)}, u32[]{:S(2)}) %collective-permute-start.1) | collective-permute-done | bytes 262176 | tf_op jit(solution)/shard_map/ppermute | solution.py:34
  35.4 9.3 %collective-permute-done.2 = f32[1,4,128,128]{3,2,1,0:T(8,128)S(1)} collective-permute-done((f32[1,4,128,128]{3,2,1,0:T(8,128)S(1)}, f32[1,4,128,128]{3,2,1,0:T(8,128)S(1)}, u32[]{:S(2)}, u32[]{:S(2)}) %collective-permute-start.2) | collective-permute-done | bytes 262176 | tf_op jit(solution)/shard_map/ppermute | solution.py:34
  44.8 9.1 %collective-permute-done.3 = f32[1,4,128,128]{3,2,1,0:T(8,128)S(1)} collective-permute-done((f32[1,4,128,128]{3,2,1,0:T(8,128)S(1)}, f32[1,4,128,128]{3,2,1,0:T(8,128)S(1)}, u32[]{:S(2)}, u32[]{:S(2)}) %collective-permute-start.3) | collective-permute-done | bytes 262176 | tf_op jit(solution)/shard_map/ppermute | solution.py:34
  53.8 0.7 copy-done.2
  54.5 1.0 iota_compare_fusion
  55.5 8.2 %collective-permute-done.4 = f32[1,4,128,128]{3,2,1,0:T(8,128)} collective-permute-done((f32[1,4,128,128]{3,2,1,0:T(8,128)S(1)}, f32[1,4,128,128]{3,2,1,0:T(8,128)}, u32[]{:S(2)}, u32[]{:S(2)}) %collective-permute-start.4) | collective-permute-done | bytes 262176 | tf_op jit(solution)/shard_map/ppermute | solution.py:34
  63.7 6.6 %fusion = f32[4,768,128]{1,2,0:T(8,128)} fusion(bf16[768,4,128]{0,2,1:T(8,128)(2,1)S(1)} %bitcast.53, f32[4,768]{1,0:T(4,128)S(1)} %get-tuple-element.8, pred[768,768]{1,0:T(8,128)(4,1)} %iota_compare_fusion, bf16[768,4,128]{0,2,1:T(8,128)(2,1)S(1)} %bitcast.51, bf16[768,512]{1,0:T(8,128)(2,1)S(1)} %copy-done), kind=kOutput, calls=%fused_computation.1 | convolution fusion | flops 1222115328 | bytes 4534272 | tf_op jit(solution)/shard_map/hts,she->the/dot_general | solution.py:28
  70.3 0.7 dynamic_slice.10
  71.0 2.4 collective-permute-done.5
  73.4 0.7 iota_compare_fusion.2
  75.5 0.7 dynamic_slice.11
  76.1 0.6 dynamic-slice
  77.3 0.2 dynamic-update-slice
  77.5 21.8 %all-reduce = f32[32]{0:T(128)S(1)} all-reduce(f32[32]{0:T(128)S(1)} %dynamic-update-slice), channel_id=2, replica_groups=mesh['seg'=8,'head'=4] {'seg'}, use_global_device_ids=true, to_apply=%add | all-reduce | flops 32 | bytes 256
  100.3 1.0 constant_dynamic-update-slice_fusion.14
  101.3 1.0 constant_dynamic-update-slice_fusion.13
  102.2 1.0 constant_dynamic-update-slice_fusion.12
  103.4 1.1 constant_dynamic-update-slice_fusion.6
  104.4 1.0 constant_dynamic-update-slice_fusion.5
  105.6 0.4 select_reduce_fusion.1
  106.0 1.1 multiply_reduce_fusion
  107.1 5.7 %psum.7 = f32[768]{0:T(1024)S(1)} all-reduce(f32[768]{0:T(1024)S(1)} %get-tuple-element.9), channel_id=1, replica_groups=mesh['seg'=8,'head'=4] {'head'}, use_global_device_ids=true, to_apply=%region_6.7 | all-reduce | flops 768 | bytes 6144 | tf_op jit(solution)/shard_map/psum | solution.py:54
  112.9 11.9 %fusion.24 = f32[768,6144]{1,0:T(8,128)} fusion(bf16[768,512]{0,1:T(8,128)(2,1)S(1)} %fusion.5, bf16[512,6144]{1,0:T(8,128)(2,1)} %param.13), kind=kOutput, calls=%fused_computation.53 | convolution fusion | flops 4831838208 | bytes 25952256 | tf_op jit(solution)/shard_map/dot_general | solution.py:59
  124.9 135.1 %reduce-scatter.2.cloned.1.call-done = f32[192,6144]{1,0:T(8,128)} async-done(((f32[768,6144]{1,0:T(8,128)}), f32[192,6144]{1,0:T(8,128)}) %reduce-scatter.2.cloned.1.call-update) | async-done | bytes 4718608 | tf_op jit(solution)/shard_map/reduce_scatter | solution.py:58
  260.0 4.1 %convert_element_type.17 = bf16[192,6144]{1,0:T(8,128)(2,1)} convert(f32[192,6144]{1,0:T(8,128)} %reduce-scatter.2.cloned.1.call-done) | non-fusion elementwise | flops 1179648 | bytes 7077888 | tf_op jit(solution)/shard_map/convert_element_type | solution.py:64
  (46 shorter events, 1.3 us)
Async XLA Ops:
  6.5 57.2 %copy-start = (bf16[768,512]{1,0:T(8,128)(2,1)S(1)}, bf16[768,512]{1,0:T(8,128)(2,1)}, u32[]{:S(2)}) copy-start(bf16[768,512]{1,0:T(8,128)(2,1)} %param.7) | copy-start | bytes 2359300
  6.5 253.4 %reduce-scatter.2.cloned.1.call-start = ((), (), s32[]{:S(2)}) async-start(), calls=%async_computation.1 | async-start | bytes 23592960 | tf_op jit(solution)/shard_map/reduce_scatter | solution.py:58
  12.9 12.4 %collective-permute-start = (f32[1,4,128,128]{3,2,1,0:T(8,128)S(1)}, f32[1,4,128,128]{3,2,1,0:T(8,128)S(1)}, u32[]{:S(2)}, u32[]{:S(2)}) collective-permute-start(f32[1,4,128,128]{3,2,1,0:T(8,128)S(1)} %fusion.9), channel_id=1, source_target_pairs={{0,4},{4,8},{8,12},{12,16},{16,20},{20,24},{24,28},{28,0},{1,5},{5... | collective-permute-start | bytes 786440 | tf_op jit(solution)/shard_map/ppermute | solution.py:34
  25.3 10.2 %collective-permute-start.1 = (f32[1,4,128,128]{3,2,1,0:T(8,128)S(1)}, f32[1,4,128,128]{3,2,1,0:T(8,128)S(1)}, u32[]{:S(2)}, u32[]{:S(2)}) collective-permute-start(f32[1,4,128,128]{3,2,1,0:T(8,128)S(1)} %collective-permute-done), channel_id=1, source_target_pairs={{0,4},{4,8},{8,12},{12,16},{16,20},{20,24},{24,28},{28,0},{1,5},{5... | collective-permute-start | bytes 786440 | tf_op jit(solution)/shard_map/ppermute | solution.py:34
  35.4 9.3 %collective-permute-start.2 = (f32[1,4,128,128]{3,2,1,0:T(8,128)S(1)}, f32[1,4,128,128]{3,2,1,0:T(8,128)S(1)}, u32[]{:S(2)}, u32[]{:S(2)}) collective-permute-start(f32[1,4,128,128]{3,2,1,0:T(8,128)S(1)} %collective-permute-done.1), channel_id=1, source_target_pairs={{0,4},{4,8},{8,12},{12,16},{16,20},{20,24},{24,28},{28,0},{1,5},{5... | collective-permute-start | bytes 786440 | tf_op jit(solution)/shard_map/ppermute | solution.py:34
  44.8 9.1 %collective-permute-start.3 = (f32[1,4,128,128]{3,2,1,0:T(8,128)S(1)}, f32[1,4,128,128]{3,2,1,0:T(8,128)S(1)}, u32[]{:S(2)}, u32[]{:S(2)}) collective-permute-start(f32[1,4,128,128]{3,2,1,0:T(8,128)S(1)} %collective-permute-done.2), channel_id=1, source_target_pairs={{0,4},{4,8},{8,12},{12,16},{16,20},{20,24},{24,28},{28,0},{1,5},{5... | collective-permute-start | bytes 786440 | tf_op jit(solution)/shard_map/ppermute | solution.py:34
  53.8 0.7 copy-start.2
  54.5 9.2 %collective-permute-start.4 = (f32[1,4,128,128]{3,2,1,0:T(8,128)S(1)}, f32[1,4,128,128]{3,2,1,0:T(8,128)}, u32[]{:S(2)}, u32[]{:S(2)}) collective-permute-start(f32[1,4,128,128]{3,2,1,0:T(8,128)S(1)} %collective-permute-done.3), channel_id=1, source_target_pairs={{0,4},{4,8},{8,12},{12,16},{16,20},{20,24},{24,28},{28,0},{1,5},{5... | collective-permute-start | bytes 786440 | tf_op jit(solution)/shard_map/ppermute | solution.py:34
  55.5 14.8 %copy-start.5 = (s32[8]{0:T(128)S(1)}, s32[8]{0:T(128)}, u32[]{:S(2)}) copy-start(s32[8]{0:T(128)} %param.11) | copy-start | bytes 100
  55.5 20.6 %copy-start.6 = (u32[32]{0:T(128)S(1)}, u32[32]{0:T(128)}, u32[]{:S(2)}) copy-start(u32[32]{0:T(128)} %constant.51) | copy-start | bytes 388
  63.7 9.7 %collective-permute-start.5 = (f32[1,4,128,128]{3,2,1,0:T(8,128)}, f32[1,4,128,128]{3,2,1,0:T(8,128)}, u32[]{:S(2)}, u32[]{:S(2)}) collective-permute-start(f32[1,4,128,128]{3,2,1,0:T(8,128)} %collective-permute-done.4), channel_id=1, source_target_pairs={{0,4},{4,8},{8,12},{12,16},{16,20},{20,24},{24,28},{28,0},{1,5},{5... | collective-permute-start | bytes 786440 | tf_op jit(solution)/shard_map/ppermute | solution.py:34
  70.3 35.1 %copy-start.3 = (f32[1,4,128,128]{3,2,1,0:T(8,128)S(1)}, f32[1,4,128,128]{3,2,1,0:T(8,128)}, u32[]{:S(2)}) copy-start(f32[1,4,128,128]{3,2,1,0:T(8,128)} %copy-done.2) | copy-start | bytes 786436
  73.4 26.9 %collective-permute-start.6 = (f32[1,4,128,128]{3,2,1,0:T(8,128)}, f32[1,4,128,128]{3,2,1,0:T(8,128)S(1)}, u32[]{:S(2)}, u32[]{:S(2)}) collective-permute-start(f32[1,4,128,128]{3,2,1,0:T(8,128)} %collective-permute-done.5), channel_id=1, source_target_pairs={{0,4},{4,8},{8,12},{12,16},{16,20},{20,24},{24,28},{28,0},{1,5},{5... | collective-permute-start | bytes 786440 | tf_op jit(solution)/shard_map/ppermute | solution.py:34
  103.2 2.7 %copy-start.1 = (f32[4,768,128]{1,2,0:T(8,128)S(1)}, f32[4,768,128]{1,2,0:T(8,128)}, u32[]{:S(2)}) copy-start(f32[4,768,128]{1,2,0:T(8,128)} %fusion) | copy-start | bytes 4718596
  105.5 7.2 %copy-start.4 = (f32[512]{0:T(512)S(1)}, f32[512]{0:T(512)}, u32[]{:S(2)}) copy-start(f32[512]{0:T(512)} %param.12) | copy-start | bytes 6148
Sparse Core Ops, SparseCore 0:
  125.0 134.9 reduce-scatter.1
